TPU v7x, 32 devices: a whole 2x2x4 slice. The times are simulated.
32 devices in a mesh: tm: 8 (over y, x, core), grp: 4 (over z).
Axes of the slice: x: 2, y: 2, z: 4, core: 2. Of those that a mesh axis runs over, the one named last changes fastest.
Arguments:
- series: float32 [131072, 512], P(('tm', 'grp')), may hold values from -6 to 6
- filter_taps: float32 [33], replicated, may hold values from -1 to 1
- sign_flips: int32 [131072], P(('tm', 'grp')), may hold values from -1 to 1, as said below
- samples: int32 [8192], replicated, may hold values from 0 to 131071, as said below
Outputs:
- sketch: float32 [8192, 512], P(('tm', 'grp'))
- r_factor: float32 [512, 512], replicated
Inputs may be any that keep to these rules, and one draw needn't show every extreme that they name: `sign_flips`: each entry is -1 or +1. All distinct; the values of samples modulo 4096 take exactly 4096 distinct values, each by exactly 2 consecutive entries; entries are ordered by their value modulo 4096, then by value.
All inputs are finite; a program needn't handle non-finite values.
Results may differ from a plain program's by a relative error of at most 0.0003.
Values sent between devices are 32-bit elements; how exact they have to be, the bound alone decides.
A program may use at most 128 MiB of HBM per device.

v0:
```python
import jax
import jax.numpy as jnp
from jax import lax
from jax.sharding import PartitionSpec as P


def extended(block, sides, width):
    for axis, dim in sides:
        count = lax.axis_size(axis)
        forward = [(i, i + 1) for i in range(count - 1)]
        backward = [(target, source) for source, target in forward]
        low = lax.ppermute(
            lax.slice_in_dim(block, block.shape[dim] - width, None, axis=dim), axis, forward
        )
        high = lax.ppermute(lax.slice_in_dim(block, 0, width, axis=dim), axis, backward)
        block = jnp.concatenate([low, block, high], axis=dim)
    return block


def bit_count(values, width_bits):
    counted = jnp.zeros_like(values)
    for offset in range(width_bits):
        counted = counted + (values >> offset & 1)
    return counted


def hadamard(order):
    row_ids = jnp.arange(order, dtype=jnp.int32)[:, None]
    col_ids = jnp.arange(order, dtype=jnp.int32)[None, :]
    parity = bit_count(row_ids & col_ids, max(order.bit_length(), 1)) & 1
    return (1 - 2 * parity).astype(jnp.float32)


def local_transform(rows_block):
    length, columns = rows_block.shape
    levels = length.bit_length() - 1
    outer = 2 ** ((levels + 1) // 2)
    inner = length // outer
    layered = rows_block.reshape(outer, inner, columns)
    layered = jnp.einsum("ux,xvw->uvw", hadamard(outer), layered, precision=lax.Precision.HIGHEST)
    layered = jnp.einsum("vy,uyw->uvw", hadamard(inner), layered, precision=lax.Precision.HIGHEST)
    return layered.reshape(length, columns)


def on_device(series, filter_taps, sign_flips, samples):
    rows_dev = series.shape[0]
    columns = series.shape[1]
    tap_count = filter_taps.shape[0]
    half_taps = (tap_count - 1) // 2
    devices_all = lax.axis_size("tm") * lax.axis_size("grp")
    total_rows = rows_dev * devices_all
    sample_count = samples.shape[0]
    padded = extended(series, ((("tm", "grp"), 0),), half_taps)
    filtered = filter_taps[0] * padded[0:rows_dev]
    for offset in range(1, tap_count):
        filtered = filtered + filter_taps[offset] * padded[offset : offset + rows_dev]
    flipped = filtered * sign_flips.astype(jnp.float32)[:, None]
    mixed = local_transform(flipped)
    position = lax.axis_index("tm") * lax.axis_size("grp") + lax.axis_index("grp")
    row_scale = 1.0 / jnp.sqrt(jnp.float32(total_rows))
    block_rows = sample_count // devices_all
    copies = max(2, sample_count // rows_dev)
    distinct = sample_count // copies
    per_device = distinct // devices_all
    used_positions = samples[::copies] % rows_dev
    outgoing = jnp.take(mixed, used_positions, axis=0)
    incoming = lax.all_to_all(outgoing, ("tm", "grp"), split_axis=0, concat_axis=0, tiled=True)
    stacked = incoming.reshape(devices_all, per_device, columns)
    combined = (
        jnp.einsum("op,pkw->okw", hadamard(devices_all), stacked, precision=lax.Precision.HIGHEST)
        * row_scale
    )
    combined = combined.reshape(devices_all * per_device, columns)
    mine = lax.dynamic_slice_in_dim(samples, position * block_rows, block_rows)
    slot_index = mine // rows_dev * per_device + jnp.arange(block_rows, dtype=jnp.int32) // copies
    sketch = jnp.take(combined, slot_index, axis=0)
    local_gram = lax.dot_general(
        sketch,
        sketch,
        (((0,), (0,)), ((), ())),
        precision=lax.Precision.HIGHEST,
        preferred_element_type=jnp.float32,
    )
    gram = lax.psum(local_gram, ("tm", "grp"))
    lower = jnp.linalg.cholesky(gram / sample_count)
    return (sketch, lower.T)


def solution(mesh):
    return jax.shard_map(
        on_device,
        mesh=mesh,
        in_specs=(P(("tm", "grp"), None), P(), P(("tm", "grp")), P()),
        out_specs=(P(("tm", "grp"), None), P()),
        check_vma=False,
    )
```

profile of v0, /device:TPU:0, one launch (start us, length us, event | category | flops | bytes accessed | tf_op | source)
XLA Modules:
  0.0 659.5 jit_solution(13701622514079241855)
XLA Ops:
  7.2 0.8 fusion.110
  7.9 4.9 collective-permute-start
  12.9 1.3 collective-permute-start.1
  14.2 1.4 slice.317
  15.6 2.1 fusion.111
  17.7 1.9 fusion.112
  19.6 0.7 convert_element_type.14
  20.9 11.5 %constant_dynamic-update-slice_fusion = (f32[4112,512]{1,0:T(8,128)}, f32[4112,512]{1,0:T(8,128)}) fusion(f32[4112,512]{1,0:T(8,128)} %constant_dynamic-update-slice_fusion.1, f32[4096,512]{1,0:T(8,128)} %param.4), kind=kLoop, calls=%fused_computation.143 | loop fusion | bytes 25165824 | tf_op jit(solution)/shard_map/concatenate | solution.py:16
  33.0 122.8 %fusion.1 = f32[4096,512]{1,0:T(8,128)S(1)} fusion(f32[4112,512]{1,0:T(8,128)} %constant_dynamic-update-slice_fusion.2, f32[4112,512]{1,0:T(8,128)} %get-tuple-element.10, f32[4096,512]{1,0:T(8,128)} %param.4, f32[4096]{0:T(1024)S(1)} %convert_element_type.14, f32[]{:T(128)} %bitcast.35, f32[]{:T(128)} %bitcast.34, f32[]{:T(128)} %bitcast.33, f32[]{:T(128)} %bitcast.32, ...), kind=kLoop, calls=%fused_computation.4 | loop fusion | flops 138412032 | bytes 285229184 | tf_op jit(solution)/shard_map/mul | solution.py:57
  155.8 12.4 %fusion.37 = f32[64,64,512]{2,0,1:T(8,128)S(1)} fusion(f32[64,64,512]{2,1,0:T(8,128)S(1)} %bitcast.77), kind=kOutput, calls=%fused_computation.71 | convolution fusion | flops 1610715136 | bytes 16777216 | tf_op jit(solution)/shard_map/ux,xvw->uvw/dot_general | solution.py:40
  168.3 13.8 %fusion.35 = f32[64,512,64]{1,2,0:T(8,128)} fusion(f32[64,64,512]{2,0,1:T(8,128)S(1)} %fusion.37), kind=kOutput, calls=%fused_computation.69 | convolution fusion | flops 1610715136 | bytes 16777216 | tf_op jit(solution)/shard_map/vy,uyw->uvw/dot_general | solution.py:41
  182.1 21.4 %gather_fusion = f32[4096,512]{1,0:T(8,128)} fusion(f32[4096,512]{1,0:T(8,128)} %bitcast.75, s32[4096]{0:T(1024)S(1)} %broadcast_clamp_fusion), kind=kCustom, calls=%fused_computation | custom fusion | bytes 16793600 | tf_op jit(solution)/shard_map/jit(_take)/gather | solution.py:66
  203.5 5.8 broadcast_select_fusion
  209.3 7.0 %all-to-all-start = ((f32[32,128,512]{2,1,0:T(8,128)}), f32[32,128,512]{2,1,0:T(8,128)}, u32[]{:S(2)}, u32[]{:S(2)}) async-start(f32[32,128,512]{2,1,0:T(8,128)} %broadcast_select_fusion), calls=%async_computation | async-start | bytes 16777216 | tf_op jit(solution)/shard_map/all_to_all | solution.py:67
  216.4 0.8 compare_and_fusion
  217.2 180.5 %all-to-all-done = f32[32,128,512]{2,1,0:T(8,128)} async-done(((f32[32,128,512]{2,1,0:T(8,128)}), f32[32,128,512]{2,1,0:T(8,128)}, u32[]{:S(2)}, u32[]{:S(2)}) %all-to-all-start) | async-done | bytes 8388640 | tf_op jit(solution)/shard_map/all_to_all | solution.py:67
  397.7 16.9 %broadcast_multiply_fusion = f32[32,128,512]{2,0,1:T(8,128)S(1)} fusion(f32[32,128,512]{2,1,0:T(8,128)} %all-to-all-done), kind=kOutput, calls=%fused_computation.73 | convolution fusion | flops 807426048 | bytes 16777216 | tf_op jit(solution)/shard_map/op,pkw->okw/dot_general | solution.py:70
  414.6 8.1 %copy.18 = f32[32,128,512]{2,1,0:T(8,128)} copy(f32[32,128,512]{2,0,1:T(8,128)S(1)} %broadcast_multiply_fusion) | data formatting | bytes 16777216 | tf_op jit(solution)/shard_map/mul | solution.py:70
  422.7 4.6 gather_fusion.1
  427.4 2.0 fusion.113
  429.4 134.7 %all-reduce.3.cloned.1.call-done = f32[512,512]{0,1:T(8,128)} async-done(((f32[512,512]{0,1:T(8,128)}), f32[512,512]{0,1:T(8,128)}) %all-reduce.3.cloned.1.call-update) | async-done | bytes 1048592 | tf_op jit(solution)/shard_map/psum | solution.py:84
  564.1 1.3 broadcast_multiply_fusion.1
  565.8 1.5 fusion.41
  567.3 11.7 %cholesky.104 = f32[128,128]{1,0:T(8,128)S(1)} custom-call(f32[128,128]{1,0:T(8,128)S(1)} %cholesky.266), custom_call_target="Cholesky" | custom-call | tf_op jit(solution)/shard_map/jit(cholesky)/cholesky | solution.py:85
  579.2 10.0 %custom-call.27 = f32[1,128,128]{1,2,0:T(8,128)S(1)} custom-call(f32[1,128,128]{2,1,0:T(8,128)S(1)} %get-tuple-element.23), custom_call_target="InvertDiagBlocksLowerTriangular" | custom-call | tf_op jit(solution)/shard_map/jit(cholesky)/cholesky | solution.py:85
  589.8 11.7 %cholesky.217 = f32[128,128]{1,0:T(8,128)S(1)} custom-call(f32[128,128]{1,0:T(8,128)S(1)} %cholesky.270), custom_call_target="Cholesky" | custom-call | tf_op jit(solution)/shard_map/jit(cholesky)/cholesky | solution.py:85
  601.6 9.8 %custom-call.28 = f32[1,128,128]{1,2,0:T(8,128)S(1)} custom-call(f32[1,128,128]{2,1,0:T(8,128)S(1)} %get-tuple-element.20), custom_call_target="InvertDiagBlocksLowerTriangular" | custom-call | tf_op jit(solution)/shard_map/jit(cholesky)/cholesky | solution.py:85
  612.1 11.9 %cholesky.238 = f32[128,128]{1,0:T(8,128)S(1)} custom-call(f32[128,128]{1,0:T(8,128)S(1)} %cholesky.275), custom_call_target="Cholesky" | custom-call | tf_op jit(solution)/shard_map/jit(cholesky)/cholesky | solution.py:85
  624.0 9.8 %custom-call.29 = f32[1,128,128]{1,2,0:T(8,128)S(1)} custom-call(f32[1,128,128]{2,1,0:T(8,128)S(1)} %get-tuple-element.17), custom_call_target="InvertDiagBlocksLowerTriangular" | custom-call | tf_op jit(solution)/shard_map/jit(cholesky)/cholesky | solution.py:85
  634.5 11.7 %cholesky.255 = f32[128,128]{1,0:T(8,128)S(1)} custom-call(f32[128,128]{1,0:T(8,128)S(1)} %convolution_subtract_fusion.2), custom_call_target="Cholesky" | custom-call | tf_op jit(solution)/shard_map/jit(cholesky)/cholesky | solution.py:85
  646.2 0.7 compare_reduce_fusion.1
  650.9 1.3 copy.21
  (30 shorter events, 5.3 us)
Async XLA Ops:
  7.9 12.4 %collective-permute-start = (f32[16,512]{1,0:T(8,128)S(1)}, f32[16,512]{1,0:T(8,128)S(1)}, u32[]{:S(2)}, u32[]{:S(2)}) collective-permute-start(f32[16,512]{1,0:T(8,128)S(1)} %get-tuple-element.12), channel_id=1, source_target_pairs={{0,1},{1,2},{2,3},{3,4},{4,5},{5,6},{6,7},{7,8},{8,9},{9,10},{10,1... | collective-permute-start | bytes 98312 | tf_op jit(solution)/shard_map/ppermute | solution.py:12
  12.9 19.5 %collective-permute-start.1 = (f32[16,512]{1,0:T(8,128)S(1)}, f32[16,512]{1,0:T(8,128)S(1)}, u32[]{:S(2)}, u32[]{:S(2)}) collective-permute-start(f32[16,512]{1,0:T(8,128)S(1)} %get-tuple-element.13), channel_id=1, source_target_pairs={{1,0},{2,1},{3,2},{4,3},{5,4},{6,5},{7,6},{8,7},{9,8},{10,9},{11,1... | collective-permute-start | bytes 98312 | tf_op jit(solution)/shard_map/ppermute | solution.py:15
  209.3 188.4 %all-to-all-start = ((f32[32,128,512]{2,1,0:T(8,128)}), f32[32,128,512]{2,1,0:T(8,128)}, u32[]{:S(2)}, u32[]{:S(2)}) async-start(f32[32,128,512]{2,1,0:T(8,128)} %broadcast_select_fusion), calls=%async_computation | async-start | bytes 16777216 | tf_op jit(solution)/shard_map/all_to_all | solution.py:67
  216.3 347.8 %all-reduce.3.cloned.1.call-start = ((), (), s32[]{:S(2)}) async-start(), calls=%async_computation.1 | async-start | bytes 2097152 | tf_op jit(solution)/shard_map/psum | solution.py:84
  427.4 223.5 %copy-start = (f32[256,512]{1,0:T(8,128)}, f32[256,512]{1,0:T(8,128)S(1)}, u32[]{:S(2)}) copy-start(f32[256,512]{1,0:T(8,128)S(1)} %broadcast_select_fusion.1) | copy-start | bytes 1572868
Sparse Core Ops, SparseCore 0:
  429.5 134.5 all-reduce.2
where the time goes:
time: 664 us; the launch traced here: 659 us
  waiting for transfers between devices  315 us (47%)
  other arithmetic  212 us (32%)
  local copies, waits for them, and re-layouts  54.7 us (8%)
  matrix products  47 us (7%)
  between operations  17.3 us (3%)
  starting transfers between devices  13.3 us (2%)
    all_to_all x1, waiting for transfers between devices, on_device(): lax.all_to_all(outgoing, ('tm', 'grp'), split_axis=0, concat_axis=0, tile...  181 us
    psum x1, waiting for transfers between devices, on_device(): gram = lax.psum(local_gram, ('tm', 'grp'))  135 us
    mul x1, other arithmetic, on_device(): flipped = filtered * sign_flips.astype(jnp.float32)[:, None]  123 us
    another operation x14, other arithmetic, on_device(): lower = jnp.linalg.cholesky(gram / sample_count)  78.8 us
    gather x1, local copies, waits for them, and re-layouts, on_device(): outgoing = jnp.take(mixed, used_positions, axis=0)  21.4 us
    dot_general x1, matrix products, on_device(): jnp.einsum('op,pkw->okw', hadamard(devices_all), stacked, precision=lax.P...  16.9 us
    dot_general x1, matrix products, local_transform(): jnp.einsum('vy,uyw->uvw', hadamard(inner), layered, precision=lax.Precisi...  13.8 us
  transfers between devices with their start and end apart: 4, of which 2 were waited for; matrix products, arithmetic and copies ran while one was open for 3% of the time, Pallas kernels for 0%

commit v1 on v0

--- a/solution.py
+++ b/solution.py
@@ -81,7 +81,7 @@
         precision=lax.Precision.HIGHEST,
         preferred_element_type=jnp.float32,
     )
-    gram = lax.psum(local_gram, ("tm", "grp"))
+    gram = lax.psum(lax.psum(local_gram, "grp"), "tm")
     lower = jnp.linalg.cholesky(gram / sample_count)
     return (sketch, lower.T)
 

time: 664 us -> 645 us (0.971)
  waiting for transfers between devices: 315 us -> 295 us
    psum x1 -> x2, waiting for transfers between devices: 135 us -> 115 us  [on_device(): gram = lax.psum(lax.psum(local_gram, 'grp'), 'tm')]
  transfers between devices with their start and end apart: 4 -> 5, of which waited for: 2 -> 3; matrix products, arithmetic and copies ran while one was open for 3% -> 3% of each run, Pallas kernels for 0% -> 0%
where the time goes in v1:
time: 645 us; the launch traced here: 640 us
  waiting for transfers between devices  295 us (46%)
  other arithmetic  212 us (33%)
  local copies, waits for them, and re-layouts  54.7 us (8%)
  matrix products  47.2 us (7%)
  between operations  17.3 us (3%)
  starting transfers between devices  13.6 us (2%)
    all_to_all x1, waiting for transfers between devices, on_device(): lax.all_to_all(outgoing, ('tm', 'grp'), split_axis=0, concat_axis=0, tile...  181 us
    mul x1, other arithmetic, on_device(): flipped = filtered * sign_flips.astype(jnp.float32)[:, None]  123 us
    psum x2, waiting for transfers between devices, on_device(): gram = lax.psum(lax.psum(local_gram, 'grp'), 'tm')  115 us
    another operation x14, other arithmetic, on_device(): lower = jnp.linalg.cholesky(gram / sample_count)  78.6 us
    gather x1, local copies, waits for them, and re-layouts, on_device(): outgoing = jnp.take(mixed, used_positions, axis=0)  21.4 us
    dot_general x1, matrix products, on_device(): jnp.einsum('op,pkw->okw', hadamard(devices_all), stacked, precision=lax.P...  17.3 us
    dot_general x1, matrix products, local_transform(): jnp.einsum('vy,uyw->uvw', hadamard(inner), layered, precision=lax.Precisi...  13.6 us
  transfers between devices with their start and end apart: 5, of which 3 were waited for; matrix products, arithmetic and copies ran while one was open for 3% of the time, Pallas kernels for 0%

profile of v1, /device:TPU:0, one launch (start us, length us, event | category | flops | bytes accessed | tf_op | source)
XLA Modules:
  0.0 639.8 jit_solution(9243776003949060286)
XLA Ops:
  7.2 0.8 fusion.110
  7.9 4.9 collective-permute-start
  12.9 1.3 collective-permute-start.1
  14.2 1.4 slice.317
  15.6 2.1 fusion.111
  17.7 1.9 fusion.112
  19.6 0.7 convert_element_type.14
  20.9 11.5 %constant_dynamic-update-slice_fusion = (f32[4112,512]{1,0:T(8,128)}, f32[4112,512]{1,0:T(8,128)}) fusion(f32[4112,512]{1,0:T(8,128)} %constant_dynamic-update-slice_fusion.1, f32[4096,512]{1,0:T(8,128)} %param.4), kind=kLoop, calls=%fused_computation.143 | loop fusion | bytes 25165824 | tf_op jit(solution)/shard_map/concatenate | solution.py:16
  33.0 122.8 %fusion.1 = f32[4096,512]{1,0:T(8,128)S(1)} fusion(f32[4112,512]{1,0:T(8,128)} %constant_dynamic-update-slice_fusion.2, f32[4112,512]{1,0:T(8,128)} %get-tuple-element.10, f32[4096,512]{1,0:T(8,128)} %param.4, f32[4096]{0:T(1024)S(1)} %convert_element_type.14, f32[]{:T(128)} %bitcast.35, f32[]{:T(128)} %bitcast.34, f32[]{:T(128)} %bitcast.33, f32[]{:T(128)} %bitcast.32, ...), kind=kLoop, calls=%fused_computation.4 | loop fusion | flops 138412032 | bytes 285229184 | tf_op jit(solution)/shard_map/mul | solution.py:57
  155.8 12.4 %fusion.37 = f32[64,64,512]{2,0,1:T(8,128)S(1)} fusion(f32[64,64,512]{2,1,0:T(8,128)S(1)} %bitcast.77), kind=kOutput, calls=%fused_computation.71 | convolution fusion | flops 1610715136 | bytes 16777216 | tf_op jit(solution)/shard_map/ux,xvw->uvw/dot_general | solution.py:40
  168.3 13.6 %fusion.35 = f32[64,512,64]{1,2,0:T(8,128)} fusion(f32[64,64,512]{2,0,1:T(8,128)S(1)} %fusion.37), kind=kOutput, calls=%fused_computation.69 | convolution fusion | flops 1610715136 | bytes 16777216 | tf_op jit(solution)/shard_map/vy,uyw->uvw/dot_general | solution.py:41
  181.8 21.4 %gather_fusion = f32[4096,512]{1,0:T(8,128)} fusion(f32[4096,512]{1,0:T(8,128)} %bitcast.75, s32[4096]{0:T(1024)S(1)} %broadcast_clamp_fusion), kind=kCustom, calls=%fused_computation | custom fusion | bytes 16793600 | tf_op jit(solution)/shard_map/jit(_take)/gather | solution.py:66
  203.3 5.8 broadcast_select_fusion
  209.1 7.0 %all-to-all-start = ((f32[32,128,512]{2,1,0:T(8,128)}), f32[32,128,512]{2,1,0:T(8,128)}, u32[]{:S(2)}, u32[]{:S(2)}) async-start(f32[32,128,512]{2,1,0:T(8,128)} %broadcast_select_fusion), calls=%async_computation | async-start | bytes 16777216 | tf_op jit(solution)/shard_map/all_to_all | solution.py:67
  216.2 0.8 compare_and_fusion
  217.0 180.5 %all-to-all-done = f32[32,128,512]{2,1,0:T(8,128)} async-done(((f32[32,128,512]{2,1,0:T(8,128)}), f32[32,128,512]{2,1,0:T(8,128)}, u32[]{:S(2)}, u32[]{:S(2)}) %all-to-all-start) | async-done | bytes 8388640 | tf_op jit(solution)/shard_map/all_to_all | solution.py:67
  397.5 17.3 %broadcast_multiply_fusion = f32[32,128,512]{2,0,1:T(8,128)S(1)} fusion(f32[32,128,512]{2,1,0:T(8,128)} %all-to-all-done), kind=kOutput, calls=%fused_computation.73 | convolution fusion | flops 807426048 | bytes 16777216 | tf_op jit(solution)/shard_map/op,pkw->okw/dot_general | solution.py:70
  414.8 8.1 %copy.18 = f32[32,128,512]{2,1,0:T(8,128)} copy(f32[32,128,512]{2,0,1:T(8,128)S(1)} %broadcast_multiply_fusion) | data formatting | bytes 16777216 | tf_op jit(solution)/shard_map/mul | solution.py:70
  422.9 4.6 gather_fusion.1
  427.6 2.0 fusion.113
  429.9 55.6 %all-reduce.4.cloned.1.call-done = f32[512,512]{0,1:T(8,128)} async-done(((f32[512,512]{0,1:T(8,128)}), f32[512,512]{0,1:T(8,128)}) %all-reduce.4.cloned.1.call-update) | async-done | bytes 1048592 | tf_op jit(solution)/shard_map/psum | solution.py:84
  485.5 59.1 %all-reduce.6.cloned.1.call-done = f32[512,512]{0,1:T(8,128)} async-done(((f32[512,512]{0,1:T(8,128)}), f32[512,512]{0,1:T(8,128)}) %all-reduce.6.cloned.1.call-update) | async-done | bytes 1048592 | tf_op jit(solution)/shard_map/psum | solution.py:84
  544.6 1.3 broadcast_multiply_fusion.1
  546.3 1.5 fusion.41
  547.8 11.7 %cholesky.104 = f32[128,128]{1,0:T(8,128)S(1)} custom-call(f32[128,128]{1,0:T(8,128)S(1)} %cholesky.266), custom_call_target="Cholesky" | custom-call | tf_op jit(solution)/shard_map/jit(cholesky)/cholesky | solution.py:85
  559.7 9.8 %custom-call.27 = f32[1,128,128]{1,2,0:T(8,128)S(1)} custom-call(f32[1,128,128]{2,1,0:T(8,128)S(1)} %get-tuple-element.23), custom_call_target="InvertDiagBlocksLowerTriangular" | custom-call | tf_op jit(solution)/shard_map/jit(cholesky)/cholesky | solution.py:85
  570.1 11.7 %cholesky.217 = f32[128,128]{1,0:T(8,128)S(1)} custom-call(f32[128,128]{1,0:T(8,128)S(1)} %cholesky.270), custom_call_target="Cholesky" | custom-call | tf_op jit(solution)/shard_map/jit(cholesky)/cholesky | solution.py:85
  581.9 10.0 %custom-call.28 = f32[1,128,128]{1,2,0:T(8,128)S(1)} custom-call(f32[1,128,128]{2,1,0:T(8,128)S(1)} %get-tuple-element.20), custom_call_target="InvertDiagBlocksLowerTriangular" | custom-call | tf_op jit(solution)/shard_map/jit(cholesky)/cholesky | solution.py:85
  592.6 11.7 %cholesky.238 = f32[128,128]{1,0:T(8,128)S(1)} custom-call(f32[128,128]{1,0:T(8,128)S(1)} %cholesky.275), custom_call_target="Cholesky" | custom-call | tf_op jit(solution)/shard_map/jit(cholesky)/cholesky | solution.py:85
  604.3 9.8 %custom-call.29 = f32[1,128,128]{1,2,0:T(8,128)S(1)} custom-call(f32[1,128,128]{2,1,0:T(8,128)S(1)} %get-tuple-element.17), custom_call_target="InvertDiagBlocksLowerTriangular" | custom-call | tf_op jit(solution)/shard_map/jit(cholesky)/cholesky | solution.py:85
  614.8 11.7 %cholesky.255 = f32[128,128]{1,0:T(8,128)S(1)} custom-call(f32[128,128]{1,0:T(8,128)S(1)} %convolution_subtract_fusion.2), custom_call_target="Cholesky" | custom-call | tf_op jit(solution)/shard_map/jit(cholesky)/cholesky | solution.py:85
  631.2 1.3 copy.21
  (33 shorter events, 6.3 us)
Async XLA Ops:
  7.9 12.4 %collective-permute-start = (f32[16,512]{1,0:T(8,128)S(1)}, f32[16,512]{1,0:T(8,128)S(1)}, u32[]{:S(2)}, u32[]{:S(2)}) collective-permute-start(f32[16,512]{1,0:T(8,128)S(1)} %get-tuple-element.12), channel_id=1, source_target_pairs={{0,1},{1,2},{2,3},{3,4},{4,5},{5,6},{6,7},{7,8},{8,9},{9,10},{10,1... | collective-permute-start | bytes 98312 | tf_op jit(solution)/shard_map/ppermute | solution.py:12
  12.9 19.5 %collective-permute-start.1 = (f32[16,512]{1,0:T(8,128)S(1)}, f32[16,512]{1,0:T(8,128)S(1)}, u32[]{:S(2)}, u32[]{:S(2)}) collective-permute-start(f32[16,512]{1,0:T(8,128)S(1)} %get-tuple-element.13), channel_id=1, source_target_pairs={{1,0},{2,1},{3,2},{4,3},{5,4},{6,5},{7,6},{8,7},{9,8},{10,9},{11,1... | collective-permute-start | bytes 98312 | tf_op jit(solution)/shard_map/ppermute | solution.py:15
  209.1 188.4 %all-to-all-start = ((f32[32,128,512]{2,1,0:T(8,128)}), f32[32,128,512]{2,1,0:T(8,128)}, u32[]{:S(2)}, u32[]{:S(2)}) async-start(f32[32,128,512]{2,1,0:T(8,128)} %broadcast_select_fusion), calls=%async_computation | async-start | bytes 16777216 | tf_op jit(solution)/shard_map/all_to_all | solution.py:67
  216.1 269.3 %all-reduce.4.cloned.1.call-start = ((), (), s32[]{:S(2)}) async-start(), calls=%async_computation.1 | async-start | bytes 2097152 | tf_op jit(solution)/shard_map/psum | solution.py:84
  427.6 203.6 %copy-start = (f32[256,512]{1,0:T(8,128)}, f32[256,512]{1,0:T(8,128)S(1)}, u32[]{:S(2)}) copy-start(f32[256,512]{1,0:T(8,128)S(1)} %broadcast_select_fusion.1) | copy-start | bytes 1572868
  429.7 115.0 %all-reduce.6.cloned.1.call-start = ((), (), s32[]{:S(2)}) async-start(), calls=%async_computation.2 | async-start | bytes 2097152 | tf_op jit(solution)/shard_map/psum | solution.py:84
Sparse Core Ops, SparseCore 0:
  429.8 55.6 all-reduce.3
  488.6 55.9 all-reduce.5
